TPU v7x, 32 devices: a whole 2x2x4 slice. The times are simulated.
32 devices in a mesh: groups: 2 (over y), lat: 8 (over z, x), lon: 2 (over core).
Axes of the slice: x: 2, y: 2, z: 4, core: 2. Of those that a mesh axis runs over, the one named last changes fastest.
Arguments:
- tokens: bfloat16 [16, 256, 768], P(('groups', 'lat'), 'lon'), parts along dimension 0, may hold values from -5 to 5
- gain_attn: float32 [768], replicated, may hold values from 0.25 to 1.75
- w_qkv: bfloat16 [768, 2304], P('lat'), may hold values from -0.048353085 to 0.048353085
- key_bias: bfloat16 [8, 12, 256], P('lat', None, 'lon'), may hold values from -3 to 250
- w_out: bfloat16 [768, 768], P('lat'), may hold values from -0.21875 to 0.21875
- gain_conv: float32 [768], replicated, may hold values from 0.25 to 1.75
- w_conv: bfloat16 [2, 768, 64], replicated, may hold values from -0.75 to 0.75
- lat_taps: float32 [16, 2], replicated, may hold values from -2 to 2
- lon_half: int32 [8], P('lat'), may hold values from 1 to 128, as said below
- lat_half: int32 [8], P('lat'), may hold values from 0 to 1, as said below
- quad_off: int32 [8], P('lat'), may hold values from 0 to 13
Outputs:
- updated: bfloat16 [16, 256, 768], P(('groups', 'lat'), 'lon'), parts along dimension 0
There are 2 independent parts, one for each index of `groups`. A program takes and returns all parts, laid end to end along the dimension named above; an argument that names none is the same for every part. Nothing has to cross between parts.
Inputs may be any that keep to these rules, and one draw needn't show every extreme that they name: `lon_half`: the bands at either pole reach 128. `lat_half`: both polar bands have 1.
All inputs are finite; a program needn't handle non-finite values.
Results may differ from a plain program's by a relative error of at most 0.008.
Values may be sent and summed in bfloat16 or wider, within the bound.
A program may use at most 64 MiB of HBM per device.

v0:
```python
import jax
import jax.numpy as jnp
from jax import lax
from jax.sharding import PartitionSpec as P


def padded(cells, sides, width):
    for axis, dim in sides:
        count = lax.axis_size(axis)
        ends = count - 1
        head = lax.slice_in_dim(cells, 0, width, axis=dim)
        tail = lax.slice_in_dim(cells, cells.shape[dim] - width, cells.shape[dim], axis=dim)
        cells = jnp.concatenate(
            [
                lax.ppermute(tail, axis, [(i, (i + 1) % count) for i in range(ends)]),
                cells,
                lax.ppermute(head, axis, [((i + 1) % count, i) for i in range(ends)]),
            ],
            axis=dim,
        )
    return cells


def layer_norm(inputs, gain):
    values = inputs.astype(jnp.float32)
    average = jnp.mean(values, axis=-1, keepdims=True)
    centered = values - average
    variance = jnp.mean(centered * centered, axis=-1, keepdims=True)
    return centered * lax.rsqrt(variance + 1e-05) * gain


def group_mix(inputs, w_conv):
    basis, length, channels = inputs.shape
    group_width = w_conv.shape[2]
    groups = channels // group_width
    mixed_rows = jnp.einsum(
        "kjgc,kgce->kjge",
        inputs.reshape(basis, length, groups, group_width),
        w_conv.reshape(basis, groups, group_width, group_width),
        preferred_element_type=jnp.float32,
    )
    return mixed_rows.reshape(basis, length, channels).astype(jnp.bfloat16)


def lon_weights(row_ids, col_ids, half_width, lon_total):
    offset_lon = (
        jnp.mod(col_ids[None, :] - row_ids[:, None] + lon_total // 2, lon_total) - lon_total // 2
    )
    distance = jnp.abs(offset_lon).astype(jnp.float32)
    span_plus = (half_width + 1).astype(jnp.float32)
    tent_weight = jnp.where(
        distance <= half_width.astype(jnp.float32), (1.0 - distance / span_plus) / span_plus, 0.0
    )
    odd_weight = tent_weight * offset_lon.astype(jnp.float32) / span_plus
    return jnp.stack([tent_weight, odd_weight]).astype(jnp.bfloat16)


def start_state(query_count, head_count, head_dim):
    running_max = jnp.full((head_count, query_count), -jnp.inf, jnp.float32)
    running_sum = jnp.zeros((head_count, query_count), jnp.float32)
    running_out = jnp.zeros((query_count, head_count, head_dim), jnp.float32)
    return (running_max, running_sum, running_out)


def attend_keys(carry_state, queries, key_rows, value_rows, bias_rows, score_scale):
    key_count = key_rows.shape[0]
    for offset in range(0, key_count, 128):
        running_max, running_sum, running_out = carry_state
        key_block = key_rows[offset : offset + 128]
        value_block = value_rows[offset : offset + 128]
        bias_block = bias_rows[offset : offset + 128]
        scores = (
            jnp.einsum("qhd,khd->hqk", queries, key_block, preferred_element_type=jnp.float32)
            * score_scale
        )
        scores = scores + bias_block.T.astype(jnp.float32)[:, None, :]
        new_max = jnp.maximum(running_max, jnp.max(scores, axis=-1))
        rescale = jnp.exp(running_max - new_max)
        exp_scores = jnp.exp(scores - new_max[:, :, None])
        running_sum = running_sum * rescale + jnp.sum(exp_scores, axis=-1)
        running_out = running_out * rescale.T[:, :, None] + jnp.einsum(
            "hqk,khd->qhd",
            exp_scores.astype(jnp.bfloat16),
            value_block,
            preferred_element_type=jnp.float32,
        )
        carry_state = (new_max, running_sum, running_out)
    return carry_state


def finish_state(carry_state):
    running_max, running_sum, running_out = carry_state
    finished = running_out / running_sum.T[:, :, None]
    return finished.reshape(finished.shape[0], -1).astype(jnp.bfloat16)


def lon_conv(blended, half_width, first_col, out_cols):
    lon_total = blended.shape[1]
    block_cols = min(128, lon_total)
    block_count = lon_total // block_cols
    first_block = jnp.floor_divide(first_col - half_width, block_cols)
    last_block = jnp.floor_divide(first_col + out_cols - 1 + half_width, block_cols)
    turn_count = jnp.minimum(block_count, last_block - first_block + 1)
    row_ids = first_col + jnp.arange(out_cols, dtype=jnp.int32)

    def add_block(turn_index, running_out):
        block_at = jnp.mod(first_block + turn_index, block_count)
        lon_block = lax.dynamic_slice_in_dim(blended, block_at * block_cols, block_cols, 1)
        col_ids = block_at * block_cols + jnp.arange(block_cols, dtype=jnp.int32)
        coeffs = lon_weights(row_ids, col_ids, half_width, lon_total)
        return running_out + jnp.einsum(
            "kjc,kcd->jd", coeffs, lon_block, preferred_element_type=jnp.float32
        )

    initial = jnp.zeros((out_cols, blended.shape[2]), jnp.float32)
    return lax.fori_loop(0, turn_count, add_block, initial)


def per_device(
    tokens,
    gain_attn,
    w_qkv,
    key_bias,
    w_out,
    gain_conv,
    w_conv,
    lat_taps,
    lon_half,
    lat_half,
    quad_off,
):
    own_tokens = tokens[0]
    count_lon, model_width = own_tokens.shape
    head_count = key_bias.shape[1]
    head_dim = model_width // head_count
    score_scale = head_dim ** (-0.5)
    lon_place = lax.axis_index("lon")
    normed = layer_norm(own_tokens, gain_attn).astype(jnp.bfloat16)
    bias_rows = key_bias[0].T
    full_qkv, full_out = (
        lax.all_gather(w_qkv, "lat", axis=0, tiled=True),
        lax.all_gather(w_out, "lat", axis=0, tiled=True),
    )
    projected = jnp.dot(normed, full_qkv, preferred_element_type=jnp.float32).astype(jnp.bfloat16)
    queries = projected[:, :model_width].reshape(count_lon, head_count, head_dim)
    key_here = projected[:, model_width : 2 * model_width]
    value_here = projected[:, 2 * model_width :]
    key_piece = lax.all_gather(key_here, "lon", axis=0, tiled=True)
    value_piece = lax.all_gather(value_here, "lon", axis=0, tiled=True)
    bias_piece = lax.all_gather(bias_rows, "lon", axis=0, tiled=True)
    length = key_piece.shape[0]
    carry_state = attend_keys(
        start_state(count_lon, head_count, head_dim),
        queries,
        key_piece.reshape(length, head_count, head_dim),
        value_piece.reshape(length, head_count, head_dim),
        bias_piece,
        score_scale,
    )
    attended = finish_state(carry_state)
    branch_out = jnp.dot(attended, full_out, preferred_element_type=jnp.float32)
    middle = (own_tokens.astype(jnp.float32) + branch_out).astype(jnp.bfloat16)
    conv_in = layer_norm(middle, gain_conv).astype(jnp.bfloat16)
    stacked = padded(conv_in[None], (("lat", 0),), 1)
    lat_row = lax.axis_index("lat")
    last_band = lax.axis_size("lat") - 1
    offsets = jnp.arange(3, dtype=jnp.int32) - 1
    one_hot = (
        (quad_off[0] + offsets + 1)[:, None]
        == jnp.arange(lat_taps.shape[0], dtype=jnp.int32)[None, :]
    ).astype(jnp.float32)
    tap_vals = jnp.dot(one_hot, lat_taps, precision=lax.Precision.HIGHEST)
    tap_vals = jnp.where((jnp.abs(offsets) <= lat_half[0])[:, None], tap_vals, 0.0)
    summed = jnp.einsum(
        "rk,rjd->kjd", tap_vals, stacked.astype(jnp.float32), precision=lax.Precision.HIGHEST
    ).astype(jnp.bfloat16)
    pole_gain = jnp.where(lat_row == 0, tap_vals[0], 0.0) + jnp.where(
        lat_row == last_band, tap_vals[2], 0.0
    )
    first_col = lon_place * count_lon
    pole_rows = (pole_gain[:, None, None] * conv_in.astype(jnp.float32)[None]).astype(jnp.bfloat16)
    mixed_rows = group_mix(summed, w_conv)
    pole_mixed = group_mix(pole_rows, w_conv)
    circle_rows, pole_all = (
        lax.all_gather(mixed_rows, "lon", axis=1, tiled=True),
        lax.all_gather(pole_mixed, "lon", axis=1, tiled=True),
    )
    lon_total = circle_rows.shape[1]
    blended = (
        circle_rows.astype(jnp.float32)
        + jnp.roll(pole_all, -(lon_total // 2), axis=1).astype(jnp.float32)
    ).astype(jnp.bfloat16)
    conv_out = lon_conv(blended, lon_half[0], first_col, count_lon)
    return (middle.astype(jnp.float32) + conv_out).astype(jnp.bfloat16)[None]


def solution(mesh):
    return jax.shard_map(
        per_device,
        mesh=mesh,
        in_specs=(
            P(("groups", "lat"), "lon", None),
            P(),
            P("lat", None),
            P("lat", None, "lon"),
            P("lat", None),
            P(),
            P(),
            P(),
            P("lat"),
            P("lat"),
            P("lat"),
        ),
        out_specs=P(("groups", "lat"), "lon", None),
        check_vma=False,
    )
```

profile of v0, /device:TPU:9, one launch (start us, length us, event | category | flops | bytes accessed | tf_op | source)
XLA Modules:
  0.0 145.8 jit_solution(11945221781708907703)
XLA Ops:
  6.5 0.0 copy-start
  6.5 0.0 copy-start.1
  6.5 0.0 copy-start.3
  6.5 0.0 all-gather.3.cloned.1.call-start
  6.5 0.7 all-gather.3.cloned.1.call-update
  7.3 0.0 all-gather.5.cloned.1.call-start
  7.3 0.7 all-gather.5.cloned.1.call-update
  8.7 1.0 convert_reduce_fusion
  9.7 1.1 fusion.29
  10.9 2.5 %all_gather.23 = bf16[256,12]{0,1:T(8,128)(2,1)S(1)} all-gather(bf16[128,12]{0,1:T(8,128)(2,1)} %bitcast.119), channel_id=1, replica_groups=mesh['groups'=2,'lat'=8,'lon'=2] {'lon'}, dimensions={0}, use_global_device_ids=true | all-gather | bytes 9216 | tf_op jit(solution)/shard_map/all_gather | solution.py:150
  14.7 1.3 reshape.244
  16.0 0.0 copy-done
  16.0 0.2 convolution_select_fusion
  16.2 0.2 add_reduce_fusion
  16.4 58.0 %all-gather.3.cloned.1.call-done = bf16[768,2304]{1,0:T(8,128)(2,1)} async-done(((bf16[96,2304]{1,0:T(8,128)(2,1)}), bf16[768,2304]{1,0:T(8,128)(2,1)}) %all-gather.3.cloned.1.call-update) | async-done | bytes 3538960 | tf_op jit(solution)/shard_map/all_gather | solution.py:141
  74.4 0.0 copy-done.1
  74.4 0.0 copy-done.3
  74.4 2.7 %convolution_convert_fusion = bf16[128,2304]{1,0:T(8,128)(2,1)S(1)} fusion(bf16[768,2304]{1,0:T(8,128)(2,1)} %all-gather.3.cloned.1.call-done, bf16[1,128,768]{2,1,0:T(8,128)(2,1)S(1)} %copy-done.1, f32[768]{0:T(1024)S(1)} %copy-done.3, f32[128]{0:T(128)S(1)} %add_rsqrt_fusion.1, f32[128]{0:T(128)S(1)} %broadcast_multiply_fusion.1), kind=kOutput, calls=%fused_computation.20 | convolution fusion | flops 453771264 | bytes 4329472 | tf_op jit(solution)/shard_map/dot_general | solution.py:144
  77.1 3.7 %all_gather.22 = bf16[256,768]{1,0:T(8,128)(2,1)S(1)} all-gather(bf16[128,768]{1,0:T(8,128)(2,1)S(1)} %get-tuple-element.186), channel_id=1, replica_groups=mesh['groups'=2,'lat'=8,'lon'=2] {'lon'}, dimensions={0}, use_global_device_ids=true | all-gather | bytes 589824 | tf_op jit(solution)/shard_map/all_gather | solution.py:148
  80.8 0.2 copy.28
  81.0 0.2 copy.27
  81.2 0.2 copy.31
  81.3 2.1 %all_gather.24 = bf16[256,768]{1,0:T(8,128)(2,1)S(1)} all-gather(bf16[128,768]{1,0:T(8,128)(2,1)S(1)} %get-tuple-element.187), channel_id=1, replica_groups=mesh['groups'=2,'lat'=8,'lon'=2] {'lon'}, dimensions={0}, use_global_device_ids=true | all-gather | bytes 589824 | tf_op jit(solution)/shard_map/all_gather | solution.py:149
  83.5 0.2 copy.29
  83.6 0.2 copy.32
  83.8 0.4 fusion.58
  84.2 0.4 fusion.59
  84.7 0.3 fusion.22
  85.0 0.2 fusion.17
  85.2 0.2 fusion.18
  85.5 0.0 copy-start.2
  85.5 30.8 %all-gather.5.cloned.1.call-done = bf16[768,768]{1,0:T(8,128)(2,1)} async-done(((bf16[96,768]{1,0:T(8,128)(2,1)}), bf16[768,768]{1,0:T(8,128)(2,1)}) %all-gather.5.cloned.1.call-update) | async-done | bytes 1179664 | tf_op jit(solution)/shard_map/all_gather | solution.py:142
  116.3 1.7 %fusion.60 = (f32[128]{0:T(128)S(1)}, f32[128,768]{1,0:T(8,128)S(1)}) fusion(bf16[128,768]{0,1:T(8,128)(2,1)S(1)} %bitcast.117, bf16[768,768]{1,0:T(8,128)(2,1)} %all-gather.5.cloned.1.call-done, bf16[1,128,768]{2,1,0:T(8,128)(2,1)S(1)} %copy-done.1), kind=kOutput, calls=%fused_computation.99 | convolution fusion | flops 151486336 | bytes 1966592 | tf_op jit(solution)/shard_map/dot_general | solution.py:161
  118.0 0.2 multiply_reduce_fusion
  118.2 0.0 copy-done.2
  118.2 0.1 fusion.51
  118.3 2.2 %collective-permute-start = (bf16[1,128,768]{2,1,0:T(8,128)(2,1)S(1)}, bf16[1,128,768]{2,1,0:T(8,128)(2,1)S(1)}, u32[]{:S(2)}, u32[]{:S(2)}) collective-permute-start(bf16[1,128,768]{2,1,0:T(8,128)(2,1)S(1)} %get-tuple-element.190), channel_id=1, source_target_pairs={{0,2},{2,4},{4,6},{6,8},{8,10},{10,12},{12,14},{1,3},{3,5},{5,7},{... | collective-permute-start | bytes 589832 | tf_op jit(solution)/shard_map/ppermute | solution.py:15
  120.5 4.0 %collective-permute-start.1 = (bf16[1,128,768]{2,1,0:T(8,128)(2,1)S(1)}, bf16[1,128,768]{2,1,0:T(8,128)(2,1)S(1)}, u32[]{:S(2)}, u32[]{:S(2)}) collective-permute-start(bf16[1,128,768]{2,1,0:T(8,128)(2,1)S(1)} %get-tuple-element.190), channel_id=1, source_target_pairs={{2,0},{4,2},{6,4},{8,6},{10,8},{12,10},{14,12},{3,1},{5,3},{7,5},{... | collective-permute-start | bytes 589832 | tf_op jit(solution)/shard_map/ppermute | solution.py:17
  124.5 0.2 copy.38
  124.7 0.3 convolution_convert_fusion.2
  125.0 0.2 copy.40
  125.2 4.1 %all_gather.27 = bf16[2,256,768]{2,1,0:T(8,128)(2,1)S(1)} all-gather(bf16[2,128,768]{2,1,0:T(8,128)(2,1)S(1)} %copy.40), channel_id=1, replica_groups=mesh['groups'=2,'lat'=8,'lon'=2] {'lon'}, dimensions={1}, use_global_device_ids=true | all-gather | bytes 1179648 | tf_op jit(solution)/shard_map/all_gather | solution.py:186
  129.3 0.1 fusion.54
  129.4 0.0 collective-permute-done
  129.4 2.8 %collective-permute-done.1 = bf16[1,128,768]{2,1,0:T(8,128)(2,1)S(1)} collective-permute-done((bf16[1,128,768]{2,1,0:T(8,128)(2,1)S(1)}, bf16[1,128,768]{2,1,0:T(8,128)(2,1)S(1)}, u32[]{:S(2)}, u32[]{:S(2)}) %collective-permute-start.1) | collective-permute-done | bytes 196640 | tf_op jit(solution)/shard_map/ppermute | solution.py:17
  132.2 0.1 pad_maximum_fusion
  132.2 1.4 convolution_convert_fusion.1
  133.7 0.5 copy.35
  134.2 0.3 convolution_convert_fusion.3
  134.4 0.2 copy.37
  134.6 2.5 %all_gather.26 = bf16[2,256,768]{2,1,0:T(8,128)(2,1)S(1)} all-gather(bf16[2,128,768]{2,1,0:T(8,128)(2,1)S(1)} %copy.37), channel_id=1, replica_groups=mesh['groups'=2,'lat'=8,'lon'=2] {'lon'}, dimensions={1}, use_global_device_ids=true | all-gather | bytes 1179648 | tf_op jit(solution)/shard_map/all_gather | solution.py:185
  137.1 0.2 add_convert_fusion
  137.4 0.9 while.14
  137.4 0.1 fusion.78
  137.6 0.2 fusion.79
  137.8 0.1 fusion.78
  138.0 0.2 fusion.79
  138.3 0.7 fusion.40
  (15 shorter events, 0.2 us)
Async XLA Ops:
  6.5 9.5 %copy-start = (f32[16,2]{0,1:T(2,128)S(1)}, f32[16,2]{0,1:T(2,128)}, u32[]{:S(2)}) copy-start(f32[16,2]{0,1:T(2,128)} %param.20) | copy-start | bytes 388
  6.5 67.8 %copy-start.1 = (bf16[1,128,768]{2,1,0:T(8,128)(2,1)S(1)}, bf16[1,128,768]{2,1,0:T(8,128)(2,1)}, u32[]{:S(2)}) copy-start(bf16[1,128,768]{2,1,0:T(8,128)(2,1)} %param.13) | copy-start | bytes 589828
  6.5 67.8 %copy-start.3 = (f32[768]{0:T(1024)S(1)}, f32[768]{0:T(1024)}, u32[]{:S(2)}) copy-start(f32[768]{0:T(1024)} %param.14) | copy-start | bytes 9220
  6.5 67.8 %all-gather.3.cloned.1.call-start = ((), (), s32[]{:S(2)}) async-start(), calls=%async_computation | async-start | bytes 3981312 | tf_op jit(solution)/shard_map/all_gather | solution.py:141
  7.3 109.0 %all-gather.5.cloned.1.call-start = ((), (), s32[]{:S(2)}) async-start(), calls=%async_computation.1 | async-start | bytes 1327104 | tf_op jit(solution)/shard_map/all_gather | solution.py:142
  85.5 32.7 %copy-start.2 = (f32[768]{0:T(1024)S(1)}, f32[768]{0:T(1024)}, u32[]{:S(2)}) copy-start(f32[768]{0:T(1024)} %param.18) | copy-start | bytes 9220
  118.3 11.1 %collective-permute-start = (bf16[1,128,768]{2,1,0:T(8,128)(2,1)S(1)}, bf16[1,128,768]{2,1,0:T(8,128)(2,1)S(1)}, u32[]{:S(2)}, u32[]{:S(2)}) collective-permute-start(bf16[1,128,768]{2,1,0:T(8,128)(2,1)S(1)} %get-tuple-element.190), channel_id=1, source_target_pairs={{0,2},{2,4},{4,6},{6,8},{8,10},{10,12},{12,14},{1,3},{3,5},{5,7},{... | collective-permute-start | bytes 589832 | tf_op jit(solution)/shard_map/ppermute | solution.py:15
  120.5 11.6 %collective-permute-start.1 = (bf16[1,128,768]{2,1,0:T(8,128)(2,1)S(1)}, bf16[1,128,768]{2,1,0:T(8,128)(2,1)S(1)}, u32[]{:S(2)}, u32[]{:S(2)}) collective-permute-start(bf16[1,128,768]{2,1,0:T(8,128)(2,1)S(1)} %get-tuple-element.190), channel_id=1, source_target_pairs={{2,0},{4,2},{6,4},{8,6},{10,8},{12,10},{14,12},{3,1},{5,3},{7,5},{... | collective-permute-start | bytes 589832 | tf_op jit(solution)/shard_map/ppermute | solution.py:17
Sparse Core Ops, SparseCore 0:
  9.5 64.7 all-gather.2
  76.6 39.6 all-gather.4
where the time goes:
time: 146 us
  waiting for transfers between devices  92.9 us (64%)
  between operations  15.7 us (11%)
  blocking collectives  14.8 us (10%)
  matrix products  8.42 us (6%)
  starting transfers between devices  6.22 us (4%)
  other arithmetic  4.29 us (3%)
  local copies, waits for them, and re-layouts  3.28 us (2%)
    all_gather x1, waiting for transfers between devices, per_device(): lax.all_gather(w_qkv, 'lat', axis=0, tiled=True)  58 us
    all_gather x1, waiting for transfers between devices, per_device(): lax.all_gather(w_out, 'lat', axis=0, tiled=True)  30.8 us
    all_gather x1, blocking collectives, per_device(): lax.all_gather(pole_mixed, 'lon', axis=1, tiled=True)  4.1 us
    ppermute x1, starting transfers between devices, padded(): lax.ppermute(head, axis, [((i + 1) % count, i) for i in range(ends)])  4 us
    all_gather x1, blocking collectives, per_device(): key_piece = lax.all_gather(key_here, 'lon', axis=0, tiled=True)  3.68 us
  transfers between devices with their start and end apart: 4, of which 3 were waited for; matrix products, arithmetic and copies ran while one was open for 7% of the time, Pallas kernels for 0%

commit v1 on v0

--- a/solution.py
+++ b/solution.py
@@ -2,6 +2,28 @@
 import jax.numpy as jnp
 from jax import lax
 from jax.sharding import PartitionSpec as P
+
+
+def laid_out(tiles, dim):
+    dims = list(tiles.shape[1:])
+    dims[dim] *= tiles.shape[0]
+    return jnp.moveaxis(tiles, 0, dim).reshape(dims)
+
+
+def collect(x, axis, dim):
+    devices = lax.axis_size(axis)
+    pairs = [(i, (i + 1) % devices) for i in range(devices)]
+    back = [(b, a) for a, b in pairs]
+    lower, upper = ([], [])
+    for hop in range(devices - 1):
+        if hop % 2 == 0:
+            lower.append(lax.ppermute(lower[-1] if lower else x, axis, pairs))
+        else:
+            upper.append(lax.ppermute(upper[-1] if upper else x, axis, back))
+    pieces = jnp.stack([*lower[::-1], x, *upper])
+    shift = lax.axis_index(axis) - len(lower)
+    pieces = pieces[(jnp.arange(devices) - shift) % devices]
+    return laid_out(pieces, dim)
 
 
 def padded(cells, sides, width):
@@ -139,7 +161,7 @@
     bias_rows = key_bias[0].T
     full_qkv, full_out = (
         lax.all_gather(w_qkv, "lat", axis=0, tiled=True),
-        lax.all_gather(w_out, "lat", axis=0, tiled=True),
+        collect(w_out, "lat", 0),
     )
     projected = jnp.dot(normed, full_qkv, preferred_element_type=jnp.float32).astype(jnp.bfloat16)
     queries = projected[:, :model_width].reshape(count_lon, head_count, head_dim)

time: 146 us -> 119 us (0.82)
  waiting for transfers between devices: 92.9 us -> 59.6 us
  starting transfers between devices: 6.22 us -> 13.8 us
    all_gather x1 -> x0, waiting for transfers between devices: 30.8 us -> none  [per_device(): lax.all_gather(w_out, 'lat', axis=0, tiled=True)]
    all_gather x1, waiting for transfers between devices: 58 us -> 37.6 us  [per_device(): lax.all_gather(w_qkv, 'lat', axis=0, tiled=True)]
    ppermute x0 -> x7, waiting for transfers between devices: none -> 17.4 us  [the longest x4 14.9 us: collect(): lower.append(lax.ppermute(lower[-1] if lower else x, axis, pairs))]
    ppermute x0 -> x7, starting transfers between devices: none -> 7.61 us  [the longest x3 4.6 us: collect(): upper.append(lax.ppermute(upper[-1] if upper else x, axis, back))]
  transfers between devices with their start and end apart: 4 -> 10, of which waited for: 3 -> 6; matrix products, arithmetic and copies ran while one was open for 7% -> 4% of each run, Pallas kernels for 0% -> 0%
where the time goes in v1:
time: 119 us
  waiting for transfers between devices  59.6 us (50%)
  between operations  15.8 us (13%)
  blocking collectives  14.2 us (12%)
  starting transfers between devices  13.8 us (12%)
  matrix products  7.15 us (6%)
  other arithmetic  4.34 us (4%)
  local copies, waits for them, and re-layouts  4.02 us (3%)
    all_gather x1, waiting for transfers between devices, per_device(): lax.all_gather(w_qkv, 'lat', axis=0, tiled=True)  37.6 us
    ppermute x4, waiting for transfers between devices, collect(): lower.append(lax.ppermute(lower[-1] if lower else x, axis, pairs))  14.9 us
    ppermute x3, starting transfers between devices, collect(): upper.append(lax.ppermute(upper[-1] if upper else x, axis, back))  4.6 us
    ppermute x1, waiting for transfers between devices, padded(): lax.ppermute(head, axis, [((i + 1) % count, i) for i in range(ends)])  3.93 us
    all_gather x1, blocking collectives, per_device(): key_piece = lax.all_gather(key_here, 'lon', axis=0, tiled=True)  3.68 us
    ppermute x1, starting transfers between devices, padded(): lax.ppermute(head, axis, [((i + 1) % count, i) for i in range(ends)])  3.14 us
    ppermute x1, starting transfers between devices, padded(): lax.ppermute(tail, axis, [(i, (i + 1) % count) for i in range(ends)])  3.04 us
    all_gather x1, blocking collectives, per_device(): bias_piece = lax.all_gather(bias_rows, 'lon', axis=0, tiled=True)  3.02 us
  transfers between devices with their start and end apart: 10, of which 6 were waited for; matrix products, arithmetic and copies ran while one was open for 4% of the time, Pallas kernels for 0%

profile of v1, /device:TPU:9, one launch (start us, length us, event | category | flops | bytes accessed | tf_op | source)
XLA Modules:
  0.0 119.1 jit_solution(9071557607907208161)
XLA Ops:
  6.5 0.7 all-gather.2.cloned.1.call-update
  7.3 1.3 %collective-permute-start = (bf16[96,768]{1,0:T(8,128)(2,1)}, bf16[96,768]{1,0:T(8,128)(2,1)S(1)}, u32[]{:S(2)}, u32[]{:S(2)}) collective-permute-start(bf16[96,768]{1,0:T(8,128)(2,1)} %param.17), channel_id=1, source_target_pairs={{0,2},{2,4},{4,6},{6,8},{8,10},{10,12},{12,14},{14,0},{1,3},{3,5},... | collective-permute-start | bytes 442376 | tf_op jit(solution)/shard_map/ppermute | solution.py:20
  8.5 1.2 collective-permute-start.4
  11.0 3.0 %all_gather.20 = bf16[256,12]{0,1:T(8,128)(2,1)S(1)} all-gather(bf16[128,12]{0,1:T(8,128)(2,1)} %bitcast.139), channel_id=1, replica_groups=mesh['groups'=2,'lat'=8,'lon'=2] {'lon'}, dimensions={0}, use_global_device_ids=true | all-gather | bytes 9216 | tf_op jit(solution)/shard_map/all_gather | solution.py:172
  14.0 0.2 convolution_select_fusion
  14.2 1.1 convert_reduce_fusion
  15.3 0.0 collective-permute-done
  15.3 0.4 collective-permute-start.1
  15.7 1.1 fusion.29
  16.8 4.2 %collective-permute-done.1 = bf16[96,768]{1,0:T(8,128)(2,1)S(1)} collective-permute-done((bf16[96,768]{1,0:T(8,128)(2,1)S(1)}, bf16[96,768]{1,0:T(8,128)(2,1)S(1)}, u32[]{:S(2)}, u32[]{:S(2)}) %collective-permute-start.1) | collective-permute-done | bytes 147488 | tf_op jit(solution)/shard_map/ppermute | solution.py:20
  21.0 0.0 collective-permute-start.2
  21.0 0.0 collective-permute-done.4
  21.0 2.4 %collective-permute-start.5 = (bf16[96,768]{1,0:T(8,128)(2,1)S(1)}, bf16[96,768]{1,0:T(8,128)(2,1)S(1)}, u32[]{:S(2)}, u32[]{:S(2)}) collective-permute-start(bf16[96,768]{1,0:T(8,128)(2,1)S(1)} %collective-permute-done.4), channel_id=1, source_target_pairs={{2,0},{4,2},{6,4},{8,6},{10,8},{12,10},{14,12},{0,14},{3,1},{5,3},... | collective-permute-start | bytes 442376 | tf_op jit(solution)/shard_map/ppermute | solution.py:22
  23.4 6.6 %collective-permute-done.2 = bf16[96,768]{1,0:T(8,128)(2,1)S(1)} collective-permute-done((bf16[96,768]{1,0:T(8,128)(2,1)S(1)}, bf16[96,768]{1,0:T(8,128)(2,1)S(1)}, u32[]{:S(2)}, u32[]{:S(2)}) %collective-permute-start.2) | collective-permute-done | bytes 147488 | tf_op jit(solution)/shard_map/ppermute | solution.py:20
  30.0 1.4 %collective-permute-start.3 = (bf16[96,768]{1,0:T(8,128)(2,1)S(1)}, bf16[96,768]{1,0:T(8,128)(2,1)S(1)}, u32[]{:S(2)}, u32[]{:S(2)}) collective-permute-start(bf16[96,768]{1,0:T(8,128)(2,1)S(1)} %collective-permute-done.2), channel_id=1, source_target_pairs={{0,2},{2,4},{4,6},{6,8},{8,10},{10,12},{12,14},{14,0},{1,3},{3,5},... | collective-permute-start | bytes 442376 | tf_op jit(solution)/shard_map/ppermute | solution.py:20
  32.0 1.3 %reshape.297 = bf16[2,12,64,64]{2,1,3,0:T(8,128)(2,1)S(1)} reshape(bf16[2,768,64]{1,2,0:T(8,128)(2,1)} %param.19) | data formatting | bytes 393216 | tf_op jit(solution)/shard_map/reshape | solution.py:61
  33.4 0.2 add_reduce_fusion
  33.6 0.0 collective-permute-done.5
  33.6 1.0 collective-permute-start.6
  34.6 4.2 %collective-permute-done.3 = bf16[96,768]{1,0:T(8,128)(2,1)S(1)} collective-permute-done((bf16[96,768]{1,0:T(8,128)(2,1)S(1)}, bf16[96,768]{1,0:T(8,128)(2,1)S(1)}, u32[]{:S(2)}, u32[]{:S(2)}) %collective-permute-start.3) | collective-permute-done | bytes 147488 | tf_op jit(solution)/shard_map/ppermute | solution.py:20
  38.9 2.5 %collective-permute-done.6 = bf16[96,768]{1,0:T(8,128)(2,1)S(1)} collective-permute-done((bf16[96,768]{1,0:T(8,128)(2,1)S(1)}, bf16[96,768]{1,0:T(8,128)(2,1)S(1)}, u32[]{:S(2)}, u32[]{:S(2)}) %collective-permute-start.6) | collective-permute-done | bytes 147488 | tf_op jit(solution)/shard_map/ppermute | solution.py:22
  41.4 0.0 copy-start.1
  41.4 0.0 copy-start.4
  41.4 0.6 gather_fusion
  42.1 37.6 %all-gather.2.cloned.1.call-done = bf16[768,2304]{1,0:T(8,128)(2,1)} async-done(((bf16[96,2304]{1,0:T(8,128)(2,1)}), bf16[768,2304]{1,0:T(8,128)(2,1)}) %all-gather.2.cloned.1.call-update) | async-done | bytes 3538960 | tf_op jit(solution)/shard_map/all_gather | solution.py:163
  79.7 2.7 %convolution_convert_fusion = bf16[128,2304]{1,0:T(8,128)(2,1)S(1)} fusion(bf16[768,2304]{1,0:T(8,128)(2,1)} %all-gather.2.cloned.1.call-done, bf16[1,128,768]{2,1,0:T(8,128)(2,1)S(1)} %copy-done.1, f32[768]{0:T(1024)S(1)} %copy-done.4, f32[128]{0:T(128)S(1)} %add_rsqrt_fusion.1, f32[128]{0:T(128)S(1)} %broadcast_multiply_fusion.1), kind=kOutput, calls=%fused_computation.21 | convolution fusion | flops 453771264 | bytes 4329472 | tf_op jit(solution)/shard_map/dot_general | solution.py:166
  82.4 3.7 %all_gather.19 = bf16[256,768]{1,0:T(8,128)(2,1)S(1)} all-gather(bf16[128,768]{1,0:T(8,128)(2,1)S(1)} %get-tuple-element.186), channel_id=1, replica_groups=mesh['groups'=2,'lat'=8,'lon'=2] {'lon'}, dimensions={0}, use_global_device_ids=true | all-gather | bytes 589824 | tf_op jit(solution)/shard_map/all_gather | solution.py:170
  86.1 0.2 copy.28
  86.3 0.2 copy.27
  86.4 0.2 copy.31
  86.6 2.1 %all_gather.21 = bf16[256,768]{1,0:T(8,128)(2,1)S(1)} all-gather(bf16[128,768]{1,0:T(8,128)(2,1)S(1)} %get-tuple-element.187), channel_id=1, replica_groups=mesh['groups'=2,'lat'=8,'lon'=2] {'lon'}, dimensions={0}, use_global_device_ids=true | all-gather | bytes 589824 | tf_op jit(solution)/shard_map/all_gather | solution.py:171
  88.7 0.2 copy.29
  88.9 0.2 copy.32
  89.1 0.4 fusion.60
  89.5 0.4 fusion.61
  89.9 0.3 fusion.22
  90.2 0.2 fusion.17
  90.5 0.2 fusion.18
  90.8 0.0 copy-start.3
  90.8 0.4 fusion.62
  91.2 0.2 multiply_reduce_fusion
  91.4 0.0 copy-done.3
  91.4 0.1 fusion.53
  91.6 3.0 %collective-permute-start.7 = (bf16[1,128,768]{2,1,0:T(8,128)(2,1)S(1)}, bf16[1,128,768]{2,1,0:T(8,128)(2,1)S(1)}, u32[]{:S(2)}, u32[]{:S(2)}) collective-permute-start(bf16[1,128,768]{2,1,0:T(8,128)(2,1)S(1)} %get-tuple-element.190), channel_id=1, source_target_pairs={{0,2},{2,4},{4,6},{6,8},{8,10},{10,12},{12,14},{1,3},{3,5},{5,7},{... | collective-permute-start | bytes 589832 | tf_op jit(solution)/shard_map/ppermute | solution.py:37
  94.6 3.1 %collective-permute-start.8 = (bf16[1,128,768]{2,1,0:T(8,128)(2,1)S(1)}, bf16[1,128,768]{2,1,0:T(8,128)(2,1)S(1)}, u32[]{:S(2)}, u32[]{:S(2)}) collective-permute-start(bf16[1,128,768]{2,1,0:T(8,128)(2,1)S(1)} %get-tuple-element.190), channel_id=1, source_target_pairs={{2,0},{4,2},{6,4},{8,6},{10,8},{12,10},{14,12},{3,1},{5,3},{7,5},{... | collective-permute-start | bytes 589832 | tf_op jit(solution)/shard_map/ppermute | solution.py:39
  97.8 0.2 copy.38
  97.9 0.3 convolution_convert_fusion.2
  98.3 0.2 copy.40
  98.5 2.9 %all_gather.23 = bf16[2,256,768]{2,1,0:T(8,128)(2,1)S(1)} all-gather(bf16[2,128,768]{2,1,0:T(8,128)(2,1)S(1)} %copy.40), channel_id=1, replica_groups=mesh['groups'=2,'lat'=8,'lon'=2] {'lon'}, dimensions={1}, use_global_device_ids=true | all-gather | bytes 1179648 | tf_op jit(solution)/shard_map/all_gather | solution.py:208
  101.4 0.1 fusion.56
  101.5 3.9 %collective-permute-done.8 = bf16[1,128,768]{2,1,0:T(8,128)(2,1)S(1)} collective-permute-done((bf16[1,128,768]{2,1,0:T(8,128)(2,1)S(1)}, bf16[1,128,768]{2,1,0:T(8,128)(2,1)S(1)}, u32[]{:S(2)}, u32[]{:S(2)}) %collective-permute-start.8) | collective-permute-done | bytes 196640 | tf_op jit(solution)/shard_map/ppermute | solution.py:39
  105.4 0.1 pad_maximum_fusion
  105.5 1.4 %convolution_convert_fusion.1 = bf16[2,128,768]{2,0,1:T(2,128)(2,1)S(1)} fusion(bf16[3,128,768]{2,1,0:T(8,128)(2,1)S(1)} %pad_maximum_fusion, f32[3,2]{0,1:T(2,128)S(1)} %convolution_select_fusion), kind=kOutput, calls=%fused_computation.27 | convolution fusion | flops 7274496 | bytes 983064 | tf_op jit(solution)/shard_map/rk,rjd->kjd/dot_general | solution.py:196
  106.9 0.5 copy.35
  107.4 0.3 convolution_convert_fusion.3
  107.7 0.2 copy.37
  107.9 2.5 %all_gather.22 = bf16[2,256,768]{2,1,0:T(8,128)(2,1)S(1)} all-gather(bf16[2,128,768]{2,1,0:T(8,128)(2,1)S(1)} %copy.37), channel_id=1, replica_groups=mesh['groups'=2,'lat'=8,'lon'=2] {'lon'}, dimensions={1}, use_global_device_ids=true | all-gather | bytes 1179648 | tf_op jit(solution)/shard_map/all_gather | solution.py:207
  110.4 0.2 add_convert_fusion
  110.6 0.9 while.14
  110.7 0.1 fusion.80
  110.8 0.2 fusion.81
  111.1 0.1 fusion.80
  111.2 0.2 fusion.81
  111.5 0.7 fusion.40
  (33 shorter events, 0.3 us)
Async XLA Ops:
  6.5 7.5 %copy-start = (f32[16,2]{0,1:T(2,128)S(1)}, f32[16,2]{0,1:T(2,128)}, u32[]{:S(2)}) copy-start(f32[16,2]{0,1:T(2,128)} %param.20) | copy-start | bytes 388
  6.5 73.1 %all-gather.2.cloned.1.call-start = ((), (), s32[]{:S(2)}) async-start(), calls=%async_computation | async-start | bytes 3981312 | tf_op jit(solution)/shard_map/all_gather | solution.py:163
  7.3 8.0 %collective-permute-start = (bf16[96,768]{1,0:T(8,128)(2,1)}, bf16[96,768]{1,0:T(8,128)(2,1)S(1)}, u32[]{:S(2)}, u32[]{:S(2)}) collective-permute-start(bf16[96,768]{1,0:T(8,128)(2,1)} %param.17), channel_id=1, source_target_pairs={{0,2},{2,4},{4,6},{6,8},{8,10},{10,12},{12,14},{14,0},{1,3},{3,5},... | collective-permute-start | bytes 442376 | tf_op jit(solution)/shard_map/ppermute | solution.py:20
  8.5 12.5 %collective-permute-start.4 = (bf16[96,768]{1,0:T(8,128)(2,1)}, bf16[96,768]{1,0:T(8,128)(2,1)S(1)}, u32[]{:S(2)}, u32[]{:S(2)}) collective-permute-start(bf16[96,768]{1,0:T(8,128)(2,1)} %param.17), channel_id=1, source_target_pairs={{2,0},{4,2},{6,4},{8,6},{10,8},{12,10},{14,12},{0,14},{3,1},{5,3},... | collective-permute-start | bytes 442376 | tf_op jit(solution)/shard_map/ppermute | solution.py:22
  14.2 24.7 %copy-start.2 = (bf16[96,768]{1,0:T(8,128)(2,1)S(1)}, bf16[96,768]{1,0:T(8,128)(2,1)}, u32[]{:S(2)}) copy-start(bf16[96,768]{1,0:T(8,128)(2,1)} %param.17) | copy-start | bytes 442372
  15.3 5.6 %collective-permute-start.1 = (bf16[96,768]{1,0:T(8,128)(2,1)S(1)}, bf16[96,768]{1,0:T(8,128)(2,1)S(1)}, u32[]{:S(2)}, u32[]{:S(2)}) collective-permute-start(bf16[96,768]{1,0:T(8,128)(2,1)S(1)} %collective-permute-done), channel_id=1, source_target_pairs={{0,2},{2,4},{4,6},{6,8},{8,10},{10,12},{12,14},{14,0},{1,3},{3,5},... | collective-permute-start | bytes 442376 | tf_op jit(solution)/shard_map/ppermute | solution.py:20
  21.0 9.0 %collective-permute-start.2 = (bf16[96,768]{1,0:T(8,128)(2,1)S(1)}, bf16[96,768]{1,0:T(8,128)(2,1)S(1)}, u32[]{:S(2)}, u32[]{:S(2)}) collective-permute-start(bf16[96,768]{1,0:T(8,128)(2,1)S(1)} %collective-permute-done.1), channel_id=1, source_target_pairs={{0,2},{2,4},{4,6},{6,8},{8,10},{10,12},{12,14},{14,0},{1,3},{3,5},... | collective-permute-start | bytes 442376 | tf_op jit(solution)/shard_map/ppermute | solution.py:20
  21.0 12.6 %collective-permute-start.5 = (bf16[96,768]{1,0:T(8,128)(2,1)S(1)}, bf16[96,768]{1,0:T(8,128)(2,1)S(1)}, u32[]{:S(2)}, u32[]{:S(2)}) collective-permute-start(bf16[96,768]{1,0:T(8,128)(2,1)S(1)} %collective-permute-done.4), channel_id=1, source_target_pairs={{2,0},{4,2},{6,4},{8,6},{10,8},{12,10},{14,12},{0,14},{3,1},{5,3},... | collective-permute-start | bytes 442376 | tf_op jit(solution)/shard_map/ppermute | solution.py:22
  30.0 8.8 %collective-permute-start.3 = (bf16[96,768]{1,0:T(8,128)(2,1)S(1)}, bf16[96,768]{1,0:T(8,128)(2,1)S(1)}, u32[]{:S(2)}, u32[]{:S(2)}) collective-permute-start(bf16[96,768]{1,0:T(8,128)(2,1)S(1)} %collective-permute-done.2), channel_id=1, source_target_pairs={{0,2},{2,4},{4,6},{6,8},{8,10},{10,12},{12,14},{14,0},{1,3},{3,5},... | collective-permute-start | bytes 442376 | tf_op jit(solution)/shard_map/ppermute | solution.py:20
  33.6 7.8 %collective-permute-start.6 = (bf16[96,768]{1,0:T(8,128)(2,1)S(1)}, bf16[96,768]{1,0:T(8,128)(2,1)S(1)}, u32[]{:S(2)}, u32[]{:S(2)}) collective-permute-start(bf16[96,768]{1,0:T(8,128)(2,1)S(1)} %collective-permute-done.5), channel_id=1, source_target_pairs={{2,0},{4,2},{6,4},{8,6},{10,8},{12,10},{14,12},{0,14},{3,1},{5,3},... | collective-permute-start | bytes 442376 | tf_op jit(solution)/shard_map/ppermute | solution.py:22
  41.4 38.2 %copy-start.1 = (bf16[1,128,768]{2,1,0:T(8,128)(2,1)S(1)}, bf16[1,128,768]{2,1,0:T(8,128)(2,1)}, u32[]{:S(2)}) copy-start(bf16[1,128,768]{2,1,0:T(8,128)(2,1)} %param.13) | copy-start | bytes 589828
  41.4 38.2 %copy-start.4 = (f32[768]{0:T(1024)S(1)}, f32[768]{0:T(1024)}, u32[]{:S(2)}) copy-start(f32[768]{0:T(1024)} %param.14) | copy-start | bytes 9220
  90.8 0.7 copy-start.3
  91.6 9.9 %collective-permute-start.7 = (bf16[1,128,768]{2,1,0:T(8,128)(2,1)S(1)}, bf16[1,128,768]{2,1,0:T(8,128)(2,1)S(1)}, u32[]{:S(2)}, u32[]{:S(2)}) collective-permute-start(bf16[1,128,768]{2,1,0:T(8,128)(2,1)S(1)} %get-tuple-element.190), channel_id=1, source_target_pairs={{0,2},{2,4},{4,6},{6,8},{8,10},{10,12},{12,14},{1,3},{3,5},{5,7},{... | collective-permute-start | bytes 589832 | tf_op jit(solution)/shard_map/ppermute | solution.py:37
  94.6 10.8 %collective-permute-start.8 = (bf16[1,128,768]{2,1,0:T(8,128)(2,1)S(1)}, bf16[1,128,768]{2,1,0:T(8,128)(2,1)S(1)}, u32[]{:S(2)}, u32[]{:S(2)}) collective-permute-start(bf16[1,128,768]{2,1,0:T(8,128)(2,1)S(1)} %get-tuple-element.190), channel_id=1, source_target_pairs={{2,0},{4,2},{6,4},{8,6},{10,8},{12,10},{14,12},{3,1},{5,3},{7,5},{... | collective-permute-start | bytes 589832 | tf_op jit(solution)/shard_map/ppermute | solution.py:39
Sparse Core Ops, SparseCore 0:
  9.5 70.0 all-gather.1
